TPU v7x, 512 devices: a whole 4x4x16 slice. The times are simulated.
512 devices in a mesh: mode: 64 (over y, z), rank: 8 (over x, core).
Axes of the slice: x: 4, y: 4, z: 16, core: 2. Of those that a mesh axis runs over, the one named last changes fastest.
Arguments:
- operator_cores: bfloat16 [2, 4, 4, 2048, 2048], P(None, None, None, 'mode'), may hold values from -0.26516504 to 0.26516504
- vector_cores: bfloat16 [2, 64, 64, 2048], P(None, 'rank', None, 'mode'), may hold values from -17 to 17
- left_gram: float32 [256, 256], replicated, may hold values from -330 to 330, as said below
- bases: float32 [3, 256, 64], replicated, may hold values from -0.375 to 0.375
Outputs:
- rounded_cores: float32 [2, 64, 2048, 64], P(None, None, ('mode', 'rank'))
- final_gram: float32 [256, 256], replicated
Inputs may be any that keep to these rules, and one draw needn't show every extreme that they name: left_gram is symmetric positive definite.
All inputs are finite; a program needn't handle non-finite values.
Results may differ from a plain program's by a relative error of at most 0.0028.
Values may be sent and summed in bfloat16 or wider, within the bound.
A program may use at most 64 MiB of HBM per device.

v0:
```python
import jax
import jax.numpy as jnp
from jax import lax
from jax.sharding import PartitionSpec as P

MODES = 2048
RANK = 256
HIGHEST_PRECISION = lax.Precision.HIGHEST


def solve_mixing(gram_now, basis):
    projected = jnp.dot(
        basis.T, gram_now, precision=HIGHEST_PRECISION, preferred_element_type=jnp.float32
    )
    reduced = jnp.dot(
        projected, basis, precision=HIGHEST_PRECISION, preferred_element_type=jnp.float32
    )
    reduced = 0.5 * (reduced + reduced.T)
    lower_factor = jnp.linalg.cholesky(reduced)
    return jax.scipy.linalg.cho_solve((lower_factor, True), projected)


def shards(operator_cores, vector_cores, left_gram, bases):
    gram_now = left_gram
    results = []
    core_count = operator_cores.shape[0]
    for core_index in range(core_count):
        mixing = solve_mixing(gram_now, bases[core_index])
        next_basis = bases[core_index + 1]
        operator_core = operator_cores[core_index]
        vector_core = vector_cores[core_index]
        local_rows = vector_core.shape[0]
        vector_width = vector_core.shape[1]
        operator_width = operator_core.shape[0]
        local_modes = operator_core.shape[2]
        gathered = lax.all_gather(vector_core, "mode", axis=2, tiled=True)
        product = jnp.einsum(
            "qsj,ptij->qpist", gathered, operator_core, preferred_element_type=jnp.float32
        )
        row_major = product.reshape(
            local_rows * operator_width, local_modes, vector_width * operator_width
        )
        row_major = row_major.astype(jnp.bfloat16)
        exchanged = lax.all_to_all(row_major, "rank", split_axis=1, concat_axis=0, tiled=True)
        widened = exchanged.astype(jnp.float32)
        weighted = jnp.einsum("ad,dib->aib", gram_now, widened, precision=HIGHEST_PRECISION)
        partial_gram = jnp.einsum("aib,aic->bc", widened, weighted, precision=HIGHEST_PRECISION) / (
            MODES * RANK
        )
        mixed = jnp.einsum("sa,aib->sib", mixing, widened, precision=HIGHEST_PRECISION)
        rounded_core = jnp.einsum("sib,bt->sit", mixed, next_basis, precision=HIGHEST_PRECISION)
        results.append(rounded_core)
        gram_now = lax.psum(partial_gram, ("mode", "rank"))
    return (jnp.stack(results), gram_now)


def solution(mesh):
    placed = (P(None, None, None, "mode", None), P(None, "rank", None, "mode"), P(), P())
    return jax.shard_map(
        shards,
        mesh=mesh,
        in_specs=placed,
        out_specs=(P(None, None, ("mode", "rank"), None), P()),
        check_vma=False,
    )
```

profile of v0, /device:TPU:4, one launch (start us, length us, event | category | flops | bytes accessed | tf_op | source)
XLA Modules:
  0.0 1263.4 jit_solution(10983501923882909832)
XLA Ops:
  7.2 0.9 fusion.62
  8.1 0.7 copy.55
  8.9 0.7 copy.56
  9.6 1.1 fusion.43
  10.7 1.0 fusion.41
  11.9 5.8 cholesky.44
  17.8 0.7 compare_reduce_fusion.1
  19.1 4.9 custom-call.8
  24.5 138.1 %all-gather.5.cloned.1.call-done = bf16[1,8,64,2048]{2,1,0,3:T(8,128)(2,1)} async-done(((bf16[1,8,64,32]{2,1,0,3:T(8,128)(2,1)}), bf16[1,8,64,2048]{2,1,0,3:T(8,128)(2,1)}) %all-gather.5.cloned.1.call-update) | async-done | bytes 2097168 | tf_op jit(solution)/shard_map/all_gather | solution.py:36
  162.6 4.5 copy.31
  167.1 3.9 fusion.23
  171.0 1.4 copy.32
  172.4 1.8 copy.33
  174.2 4.8 all-to-all-start
  179.0 128.4 %all-gather.7.cloned.1.call-done = bf16[1,8,64,2048]{2,1,0,3:T(8,128)(2,1)} async-done(((bf16[1,8,64,32]{2,1,0,3:T(8,128)(2,1)}), bf16[1,8,64,2048]{2,1,0,3:T(8,128)(2,1)}) %all-gather.7.cloned.1.call-update) | async-done | bytes 2097168 | tf_op jit(solution)/shard_map/all_gather | solution.py:36
  307.4 4.5 copy.41
  311.8 4.9 fusion.18
  316.8 2.9 copy.42
  319.7 1.8 copy.43
  321.4 4.8 all-to-all-start.1
  326.3 0.7 convolution_bitcast_fusion
  327.0 1.5 fusion.29
  329.1 4.3 all-to-all-done.1
  333.9 451.1 %all-reduce.3.cloned.1.call-done = f32[256,256]{1,0:T(8,128)} async-done(((f32[256,256]{1,0:T(8,128)}), f32[256,256]{1,0:T(8,128)}) %all-reduce.3.cloned.1.call-update) | async-done | bytes 262160 | tf_op jit(solution)/shard_map/psum | solution.py:53
  784.9 1.3 fusion.37
  786.6 5.8 cholesky.55
  793.1 0.7 fusion.52
  793.8 4.9 custom-call.9
  800.1 1.5 fusion.28
  802.1 0.9 copy.46
  802.9 452.2 %all-reduce.5.cloned.1.call-done = f32[256,256]{1,0:T(8,128)} async-done(((f32[256,256]{1,0:T(8,128)}), f32[256,256]{1,0:T(8,128)}) %all-reduce.5.cloned.1.call-update) | async-done | bytes 262160 | tf_op jit(solution)/shard_map/psum | solution.py:53
  1255.2 1.7 copy.59
  (40 shorter events, 5.4 us)
Async XLA Ops:
  7.2 2.4 copy-start
  7.2 155.4 %all-gather.5.cloned.1.call-start = ((), (), s32[]{:S(2)}) async-start(), calls=%async_computation.4 | async-start | bytes 4259840 | tf_op jit(solution)/shard_map/all_gather | solution.py:36
  8.8 298.6 %all-gather.7.cloned.1.call-start = ((), (), s32[]{:S(2)}) async-start(), calls=%async_computation.5 | async-start | bytes 4259840 | tf_op jit(solution)/shard_map/all_gather | solution.py:36
  174.2 147.2 %all-to-all-start = ((bf16[32,32,256]{2,0,1:T(8,128)(2,1)}), bf16[32,32,256]{2,0,1:T(8,128)(2,1)S(1)}, u32[]{:S(2)}, u32[]{:S(2)}) async-start(bf16[32,32,256]{2,0,1:T(8,128)(2,1)} %copy.33), calls=%async_computation | async-start | bytes 1048576 | tf_op jit(solution)/shard_map/all_to_all | solution.py:44
  321.4 12.0 all-to-all-start.1
  326.2 458.7 %all-reduce.3.cloned.1.call-start = ((), (), s32[]{:S(2)}) async-start(), calls=%async_computation.2 | async-start | bytes 524288 | tf_op jit(solution)/shard_map/psum | solution.py:53
  327.0 6.5 copy-start.2
  328.5 926.7 %all-reduce.5.cloned.1.call-start = ((), (), s32[]{:S(2)}) async-start(), calls=%async_computation.3 | async-start | bytes 524288 | tf_op jit(solution)/shard_map/psum | solution.py:53
  784.9 14.6 %copy-start.1 = (f32[256,256]{1,0:T(8,128)S(1)}, f32[256,256]{1,0:T(8,128)}, u32[]{:S(2)}) copy-start(f32[256,256]{1,0:T(8,128)} %all-reduce.3.cloned.1.call-done) | copy-start | bytes 786436
Sparse Core Ops, SparseCore 0:
  11.5 151.0 all-gather.4
  166.1 141.1 all-gather.6
  333.1 451.7 all-reduce.2
  801.8 453.3 all-reduce.4
where the time goes:
time: 1260 us
  waiting for transfers between devices  1170 us (93%)
  other arithmetic  24.2 us (2%)
  local copies, waits for them, and re-layouts  21.9 us (2%)
  matrix products  19.1 us (2%)
  between operations  14 us (1%)
    psum x2, waiting for transfers between devices, shards(): gram_now = lax.psum(partial_gram, ('mode', 'rank'))  903 us
    all_gather x2, waiting for transfers between devices, shards(): gathered = lax.all_gather(vector_core, 'mode', axis=2, tiled=True)  267 us
  transfers between devices with their start and end apart: 6, of which 5 were waited for; matrix products, arithmetic and copies ran while one was open for 4% of the time, Pallas kernels for 0%

commit v1 on v0

--- a/solution.py
+++ b/solution.py
@@ -50,7 +50,9 @@
         mixed = jnp.einsum("sa,aib->sib", mixing, widened, precision=HIGHEST_PRECISION)
         rounded_core = jnp.einsum("sib,bt->sit", mixed, next_basis, precision=HIGHEST_PRECISION)
         results.append(rounded_core)
-        gram_now = lax.psum(partial_gram, ("mode", "rank"))
+        gram_now = partial_gram
+        for name in ("rank", "mode"):
+            gram_now = lax.psum(gram_now, name)
     return (jnp.stack(results), gram_now)
 
 

time: 1260 us -> 1030 us (0.82)
  the two profiles are of different devices: /device:TPU:4 before, /device:TPU:2 now
where the time goes in v1:
time: 1030 us
  waiting for transfers between devices  935 us (91%)
  other arithmetic  24.1 us (2%)
  local copies, waits for them, and re-layouts  21.9 us (2%)
  matrix products  20 us (2%)
  between operations  14.3 us (1%)
    psum x4, waiting for transfers between devices, shards(): gram_now = lax.psum(gram_now, name)  662 us
    all_gather x2, waiting for transfers between devices, shards(): gathered = lax.all_gather(vector_core, 'mode', axis=2, tiled=True)  267 us
  transfers between devices with their start and end apart: 8, of which 7 were waited for; matrix products, arithmetic and copies ran while one was open for 4% of the time, Pallas kernels for 0%

profile of v1, /device:TPU:2, one launch (start us, length us, event | category | flops | bytes accessed | tf_op | source)
XLA Modules:
  0.0 1025.8 jit_solution(16663849172990208656)
XLA Ops:
  7.2 0.9 fusion.62
  8.9 0.7 copy.56
  9.6 1.1 fusion.43
  10.7 1.0 fusion.41
  11.9 5.8 cholesky.44
  19.0 4.9 custom-call.8
  23.9 138.7 %all-gather.5.cloned.1.call-done = bf16[1,8,64,2048]{2,1,0,3:T(8,128)(2,1)} async-done(((bf16[1,8,64,32]{2,1,0,3:T(8,128)(2,1)}), bf16[1,8,64,2048]{2,1,0,3:T(8,128)(2,1)}) %all-gather.5.cloned.1.call-update) | async-done | bytes 2097168 | tf_op jit(solution)/shard_map/all_gather | solution.py:36
  162.6 4.5 copy.31
  167.1 3.9 fusion.23
  171.0 1.4 copy.32
  172.4 1.8 copy.33
  174.2 4.8 all-to-all-start
  179.0 128.4 %all-gather.7.cloned.1.call-done = bf16[1,8,64,2048]{2,1,0,3:T(8,128)(2,1)} async-done(((bf16[1,8,64,32]{2,1,0,3:T(8,128)(2,1)}), bf16[1,8,64,2048]{2,1,0,3:T(8,128)(2,1)}) %all-gather.7.cloned.1.call-update) | async-done | bytes 2097168 | tf_op jit(solution)/shard_map/all_gather | solution.py:36
  307.4 4.5 copy.41
  311.9 4.9 fusion.18
  316.8 2.9 copy.42
  319.7 1.8 copy.43
  321.5 4.8 all-to-all-start.1
  326.3 0.7 convolution_bitcast_fusion
  327.0 1.5 fusion.29
  329.0 6.1 all-to-all-done.1
  335.2 62.3 %all-reduce.5.cloned.1.call-done = f32[256,256]{1,0:T(8,128)} async-done(((f32[256,256]{1,0:T(8,128)}), f32[256,256]{1,0:T(8,128)}) %all-reduce.5.cloned.1.call-update) | async-done | bytes 262160 | tf_op jit(solution)/shard_map/psum | solution.py:55
  398.5 266.7 %all-reduce.7.cloned.1.call-done = f32[256,256]{1,0:T(8,128)} async-done(((f32[256,256]{1,0:T(8,128)}), f32[256,256]{1,0:T(8,128)}) %all-reduce.7.cloned.1.call-update) | async-done | bytes 262160 | tf_op jit(solution)/shard_map/psum | solution.py:55
  665.2 1.2 fusion.37
  666.9 5.8 cholesky.55
  674.0 4.9 custom-call.9
  678.9 1.5 fusion.30
  680.5 1.5 fusion.28
  682.5 67.0 %all-reduce.9.cloned.1.call-done = f32[256,256]{1,0:T(8,128)} async-done(((f32[256,256]{1,0:T(8,128)}), f32[256,256]{1,0:T(8,128)}) %all-reduce.9.cloned.1.call-update) | async-done | bytes 262160 | tf_op jit(solution)/shard_map/psum | solution.py:55
  750.3 0.9 copy.46
  751.2 266.0 %all-reduce.11.cloned.1.call-done = f32[256,256]{1,0:T(8,128)} async-done(((f32[256,256]{1,0:T(8,128)}), f32[256,256]{1,0:T(8,128)}) %all-reduce.11.cloned.1.call-update) | async-done | bytes 262160 | tf_op jit(solution)/shard_map/psum | solution.py:55
  1017.3 1.7 copy.61
  (44 shorter events, 6.8 us)
Async XLA Ops:
  7.2 2.4 copy-start
  7.2 155.5 %all-gather.5.cloned.1.call-start = ((), (), s32[]{:S(2)}) async-start(), calls=%async_computation.6 | async-start | bytes 4259840 | tf_op jit(solution)/shard_map/all_gather | solution.py:36
  8.8 298.6 %all-gather.7.cloned.1.call-start = ((), (), s32[]{:S(2)}) async-start(), calls=%async_computation.7 | async-start | bytes 4259840 | tf_op jit(solution)/shard_map/all_gather | solution.py:36
  174.2 147.2 %all-to-all-start = ((bf16[32,32,256]{2,0,1:T(8,128)(2,1)}), bf16[32,32,256]{2,0,1:T(8,128)(2,1)S(1)}, u32[]{:S(2)}, u32[]{:S(2)}) async-start(bf16[32,32,256]{2,0,1:T(8,128)(2,1)} %copy.33), calls=%async_computation | async-start | bytes 1048576 | tf_op jit(solution)/shard_map/all_to_all | solution.py:44
  321.5 13.7 %all-to-all-start.1 = ((bf16[32,32,256]{2,0,1:T(8,128)(2,1)}), bf16[32,32,256]{2,0,1:T(8,128)(2,1)S(1)}, u32[]{:S(2)}, u32[]{:S(2)}) async-start(bf16[32,32,256]{2,0,1:T(8,128)(2,1)} %copy.43), calls=%async_computation.1 | async-start | bytes 1048576 | tf_op jit(solution)/shard_map/all_to_all | solution.py:44
  326.3 71.3 %all-reduce.5.cloned.1.call-start = ((), (), s32[]{:S(2)}) async-start(), calls=%async_computation.2 | async-start | bytes 524288 | tf_op jit(solution)/shard_map/psum | solution.py:55
  327.0 71.1 %copy-start.1 = (f32[3,256,64]{1,2,0:T(8,128)S(1)}, f32[3,256,64]{1,2,0:T(8,128)}, u32[]{:S(2)}) copy-start(f32[3,256,64]{1,2,0:T(8,128)} %param.10) | copy-start | bytes 589828
  328.5 336.7 %all-reduce.7.cloned.1.call-start = ((), (), s32[]{:S(2)}) async-start(), calls=%async_computation.3 | async-start | bytes 524288 | tf_op jit(solution)/shard_map/psum | solution.py:55
  397.5 352.0 %all-reduce.9.cloned.1.call-start = ((), (), s32[]{:S(2)}) async-start(), calls=%async_computation.4 | async-start | bytes 524288 | tf_op jit(solution)/shard_map/psum | solution.py:55
  682.0 335.2 %all-reduce.11.cloned.1.call-start = ((), (), s32[]{:S(2)}) async-start(), calls=%async_computation.5 | async-start | bytes 524288 | tf_op jit(solution)/shard_map/psum | solution.py:55
Sparse Core Ops, SparseCore 0:
  11.5 151.0 all-gather.4
  166.2 141.1 all-gather.6
  330.0 67.4 all-reduce.4
  401.2 264.0 all-reduce.6
  682.1 67.3 all-reduce.8
  753.2 264.0 all-reduce.10

commit v2 on v0

--- a/solution.py
+++ b/solution.py
@@ -6,6 +6,13 @@
 MODES = 2048
 RANK = 256
 HIGHEST_PRECISION = lax.Precision.HIGHEST
+
+
+def all_by_exchange(value, name, dim):
+    size = lax.axis_size(name)
+    parts = jnp.stack([value for _ in range(size)])
+    parts = lax.all_to_all(parts, name, split_axis=0, concat_axis=0)
+    return jnp.concatenate(parts, axis=dim)
 
 
 def solve_mixing(gram_now, basis):
@@ -33,7 +40,7 @@
         vector_width = vector_core.shape[1]
         operator_width = operator_core.shape[0]
         local_modes = operator_core.shape[2]
-        gathered = lax.all_gather(vector_core, "mode", axis=2, tiled=True)
+        gathered = all_by_exchange(vector_core, "mode", 2)
         product = jnp.einsum(
             "qsj,ptij->qpist", gathered, operator_core, preferred_element_type=jnp.float32
         )

time: 1260 us -> 1220 us (0.968)
  waiting for transfers between devices: 1170 us -> 1070 us
  local copies, waits for them, and re-layouts: 21.9 us -> 56.4 us
  starting transfers between devices: 9.91 us -> 37.3 us
    all_gather x2 -> x0, waiting for transfers between devices: 267 us -> none  [shards(): gathered = lax.all_gather(vector_core, 'mode', axis=2, tiled=True)]
    all_to_all x0 -> x2, waiting for transfers between devices: none -> 161 us  [all_by_exchange(): parts = lax.all_to_all(parts, name, split_axis=0, concat_axis=0)]
    unnamed x10 -> x16, local copies, waits for them, and re-layouts: 3.88 us -> 37.5 us
    all_to_all x0 -> x2, starting transfers between devices: none -> 27.5 us  [all_by_exchange(): parts = lax.all_to_all(parts, name, split_axis=0, concat_axis=0)]
where the time goes in v2:
time: 1220 us
  waiting for transfers between devices  1070 us (88%)
  local copies, waits for them, and re-layouts  56.4 us (5%)
  starting transfers between devices  37.3 us (3%)
  other arithmetic  24.2 us (2%)
  matrix products  18 us (1%)
  between operations  14.3 us (1%)
    psum x2, waiting for transfers between devices, shards(): gram_now = lax.psum(partial_gram, ('mode', 'rank'))  902 us
    all_to_all x2, waiting for transfers between devices, all_by_exchange(): parts = lax.all_to_all(parts, name, split_axis=0, concat_axis=0)  161 us
    unnamed x16, local copies, waits for them, and re-layouts  37.5 us
    all_to_all x2, starting transfers between devices, all_by_exchange(): parts = lax.all_to_all(parts, name, split_axis=0, concat_axis=0)  27.5 us
  transfers between devices with their start and end apart: 6, of which 5 were waited for; matrix products, arithmetic and copies ran while one was open for 4% of the time, Pallas kernels for 0%

profile of v2, /device:TPU:4, one launch (start us, length us, event | category | flops | bytes accessed | tf_op | source)
XLA Modules:
  0.0 1217.3 jit_solution(1675432808739771378)
XLA Ops:
  8.1 2.9 broadcast_bitcast_fusion
  11.1 7.9 reshape.50
  18.9 18.7 %all-to-all-start.2 = ((bf16[64,2,8192]{2,1,0:T(2,128)(2,1)}), bf16[64,2,8192]{2,1,0:T(2,128)(2,1)S(1)}, u32[]{:S(2)}, u32[]{:S(2)}) async-start(bf16[64,2,8192]{2,1,0:T(2,128)(2,1)} %reshape.50), calls=%async_computation.2 | async-start | bytes 4194304 | tf_op jit(solution)/shard_map/all_to_all | solution.py:14
  37.7 2.9 broadcast_bitcast_fusion.1
  40.6 7.9 reshape.48
  48.5 86.4 %all-to-all-done.2 = bf16[64,2,8192]{2,1,0:T(2,128)(2,1)S(1)} async-done(((bf16[64,2,8192]{2,1,0:T(2,128)(2,1)}), bf16[64,2,8192]{2,1,0:T(2,128)(2,1)S(1)}, u32[]{:S(2)}, u32[]{:S(2)}) %all-to-all-start.2) | async-done | bytes 2097184 | tf_op jit(solution)/shard_map/all_to_all | solution.py:14
  134.9 8.8 all-to-all-start
  144.4 5.8 cholesky.44
  151.6 4.9 custom-call.8
  157.0 4.0 reshape.51
  161.0 3.1 bitcast_bitcast_fusion
  164.1 2.8 copy.40
  166.9 74.1 %all-to-all-done = bf16[64,2,8192]{2,1,0:T(2,128)(2,1)} async-done(((bf16[64,2,8192]{2,1,0:T(2,128)(2,1)}), bf16[64,2,8192]{2,1,0:T(2,128)(2,1)}, u32[]{:S(2)}, u32[]{:S(2)}) %all-to-all-start) | async-done | bytes 2097184 | tf_op jit(solution)/shard_map/all_to_all | solution.py:14
  241.0 8.0 reshape.49
  248.9 3.1 bitcast_bitcast_fusion.1
  254.2 2.3 fusion.15
  256.6 1.4 copy.32
  257.9 1.8 copy.33
  259.7 4.8 all-to-all-start.1
  264.5 6.1 fusion.12
  270.6 2.9 copy.42
  273.5 1.8 copy.43
  275.3 4.9 all-to-all-start.3
  281.0 1.5 fusion.19
  282.9 4.5 all-to-all-done.3
  287.9 450.4 %all-reduce.3.cloned.1.call-done = f32[256,256]{1,0:T(8,128)} async-done(((f32[256,256]{1,0:T(8,128)}), f32[256,256]{1,0:T(8,128)}) %all-reduce.3.cloned.1.call-update) | async-done | bytes 262160 | tf_op jit(solution)/shard_map/psum | solution.py:60
  739.8 5.8 cholesky.55
  747.0 4.9 custom-call.9
  752.8 1.5 fusion.20
  754.3 1.5 fusion.18
  757.1 451.7 %all-reduce.5.cloned.1.call-done = f32[256,256]{1,0:T(8,128)} async-done(((f32[256,256]{1,0:T(8,128)}), f32[256,256]{1,0:T(8,128)}) %all-reduce.5.cloned.1.call-update) | async-done | bytes 262160 | tf_op jit(solution)/shard_map/psum | solution.py:60
  1208.8 1.7 copy.59
  (46 shorter events, 12.1 us)
Async XLA Ops:
  7.2 136.6 %copy-start = (f32[256,256]{1,0:T(8,128)S(1)}, f32[256,256]{1,0:T(8,128)}, u32[]{:S(2)}) copy-start(f32[256,256]{1,0:T(8,128)} %param.9) | copy-start | bytes 786436
  18.9 116.0 %all-to-all-start.2 = ((bf16[64,2,8192]{2,1,0:T(2,128)(2,1)}), bf16[64,2,8192]{2,1,0:T(2,128)(2,1)S(1)}, u32[]{:S(2)}, u32[]{:S(2)}) async-start(bf16[64,2,8192]{2,1,0:T(2,128)(2,1)} %reshape.50), calls=%async_computation.2 | async-start | bytes 4194304 | tf_op jit(solution)/shard_map/all_to_all | solution.py:14
  40.6 103.1 %copy-start.1 = (f32[3,256,64]{1,2,0:T(8,128)S(1)}, f32[3,256,64]{1,2,0:T(8,128)}, u32[]{:S(2)}) copy-start(f32[3,256,64]{1,2,0:T(8,128)} %param.10) | copy-start | bytes 589828
  134.9 106.0 %all-to-all-start = ((bf16[64,2,8192]{2,1,0:T(2,128)(2,1)}), bf16[64,2,8192]{2,1,0:T(2,128)(2,1)}, u32[]{:S(2)}, u32[]{:S(2)}) async-start(bf16[64,2,8192]{2,1,0:T(2,128)(2,1)} %reshape.48), calls=%async_computation | async-start | bytes 4194304 | tf_op jit(solution)/shard_map/all_to_all | solution.py:14
  252.0 2.2 copy-start.3
  259.7 15.6 %all-to-all-start.1 = ((bf16[32,32,256]{2,0,1:T(8,128)(2,1)}), bf16[32,32,256]{2,0,1:T(8,128)(2,1)S(1)}, u32[]{:S(2)}, u32[]{:S(2)}) async-start(bf16[32,32,256]{2,0,1:T(8,128)(2,1)} %copy.33), calls=%async_computation.1 | async-start | bytes 1048576 | tf_op jit(solution)/shard_map/all_to_all | solution.py:51
  275.3 12.2 %copy-start.2 = (f32[3,256,64]{1,2,0:T(8,128)S(1)}, f32[3,256,64]{1,2,0:T(8,128)}, u32[]{:S(2)}) copy-start(f32[3,256,64]{1,2,0:T(8,128)} %param.10) | copy-start | bytes 589828
  275.3 12.1 all-to-all-start.3
  280.2 458.0 %all-reduce.3.cloned.1.call-start = ((), (), s32[]{:S(2)}) async-start(), calls=%async_computation.4 | async-start | bytes 524288 | tf_op jit(solution)/shard_map/psum | solution.py:60
  282.5 926.3 %all-reduce.5.cloned.1.call-start = ((), (), s32[]{:S(2)}) async-start(), calls=%async_computation.5 | async-start | bytes 524288 | tf_op jit(solution)/shard_map/psum | solution.py:60
Sparse Core Ops, SparseCore 0:
  287.1 451.1 all-reduce.2
  756.0 452.7 all-reduce.4
